TPU v7x, 256 devices: a whole 4x4x8 slice. The times are simulated.
256 devices in a mesh: dp: 32 (over y_lo, z, core), seq: 8 (over y_hi, x).
Axes of the slice: x: 4, y: 4 (y_hi: 2, y_lo: 2; y = y_hi * 2 + y_lo), z: 8, core: 2. Of those that a mesh axis runs over, the one named last changes fastest.
Arguments:
- acts: bfloat16 [32768, 4096], P(('dp', 'seq')), may hold values from -24 to 24
- grad_out: bfloat16 [32768, 4096], P('dp', 'seq'), may hold values from -6 to 6
- proj_weight: bfloat16 [4096, 4096], P('dp', 'seq'), may hold values from -0.09375 to 0.09375
Outputs:
- grad_acts: float32 [32768, 4096], P(('dp', 'seq'))
- grad_weight: float32 [4096, 4096], P('dp', 'seq')
All inputs are finite; a program needn't handle non-finite values.
Results may differ from a plain program's by a relative error of at most 0.014.
Values may be sent and summed in bfloat16 or wider, within the bound.
No kernel may reach another device: no remote copies, remote signals or barrier semaphores. Data moves between devices by JAX's collectives and lax.ppermute only.
A program may use at most 64 MiB of HBM per device.

v0:
```python
import jax
import jax.numpy as jnp
from jax import lax
from jax.sharding import PartitionSpec as P


def rounded(value):
    return lax.optimization_barrier(value.astype(jnp.bfloat16)).astype(jnp.float32)


def per_device(acts, grad_out, proj_weight):
    tok_rows = acts.shape[0]
    total_tokens = tok_rows * lax.axis_size("seq") * lax.axis_size("dp")
    full_weight = lax.all_gather(proj_weight, "dp", axis=0, tiled=True)
    whole_term = lax.dot_general(
        grad_out, full_weight, (((1,), (1,)), ((), ())), preferred_element_type=jnp.float32
    )
    summed = lax.psum_scatter(
        whole_term.astype(jnp.bfloat16), "seq", scatter_dimension=0, tiled=True
    ).astype(jnp.float32)
    gathered = lax.all_gather(acts, "seq", axis=0, tiled=True)
    local_term = None
    local_term = rounded(
        lax.dot_general(
            gathered, grad_out, (((0,), (0,)), ((), ())), preferred_element_type=jnp.float32
        )
    )
    wsummed = lax.psum_scatter(local_term, "dp", scatter_dimension=0, tiled=True)
    grad_weight = wsummed / jnp.sqrt(jnp.float32(total_tokens))
    return (summed, grad_weight)


def solution(mesh):
    in_specs = (P(("dp", "seq"), None), P("dp", "seq"), P("dp", "seq"))
    out_specs = (P(("dp", "seq"), None), P("dp", "seq"))
    return jax.shard_map(
        per_device, mesh=mesh, in_specs=in_specs, out_specs=out_specs, check_vma=False
    )
```

profile of v0, /device:TPU:4, one launch (start us, length us, event | category | flops | bytes accessed | tf_op | source)
XLA Modules:
  0.0 455.5 jit_solution(2296822489435364021)
XLA Ops:
  7.2 0.0 copy-start
  7.2 0.0 all-gather.3.cloned.1.call-start
  7.2 0.7 all-gather.3.cloned.1.call-update
  7.9 0.0 all-gather.5.cloned.1.call-start
  8.0 0.7 all-gather.5.cloned.1.call-update
  8.7 0.0 reduce-scatter.3.cloned.1.call-start
  8.7 71.0 %all-gather.3.cloned.1.call-done = bf16[4096,512]{1,0:T(8,128)(2,1)} async-done(((bf16[128,512]{1,0:T(8,128)(2,1)}), bf16[4096,512]{1,0:T(8,128)(2,1)}) %all-gather.3.cloned.1.call-update) | async-done | bytes 4194320 | tf_op jit(solution)/shard_map/all_gather | solution.py:14
  79.7 0.0 copy-done
  79.7 8.9 %convolution_convert_fusion = bf16[1024,4096]{1,0:T(8,128)(2,1)} fusion(bf16[1024,512]{1,0:T(8,128)(2,1)S(1)} %copy-done, bf16[4096,512]{1,0:T(8,128)(2,1)} %all-gather.3.cloned.1.call-done), kind=kOutput, calls=%fused_computation | convolution fusion | flops 4299161600 | bytes 13631488 | tf_op jit(solution)/shard_map/dot_general | solution.py:15
  88.6 0.0 reduce-scatter.3.cloned.1.call-update
  88.6 0.0 reduce-scatter.5.cloned.1.call-start
  88.7 105.8 %all-gather.5.cloned.1.call-done = bf16[1024,4096]{1,0:T(8,128)(2,1)} async-done(((bf16[128,4096]{1,0:T(8,128)(2,1)}), bf16[1024,4096]{1,0:T(8,128)(2,1)}) %all-gather.5.cloned.1.call-update) | async-done | bytes 8388624 | tf_op jit(solution)/shard_map/all_gather | solution.py:21
  194.5 8.4 %convolution_convert_fusion.1 = bf16[4096,512]{1,0:T(8,128)(2,1)S(1)} fusion(bf16[1024,4096]{1,0:T(8,128)(2,1)} %all-gather.5.cloned.1.call-done, bf16[1024,512]{1,0:T(8,128)(2,1)S(1)} %copy-done), kind=kOutput, calls=%fused_computation.1 | convolution fusion | flops 4297064448 | bytes 13631488 | tf_op jit(solution)/shard_map/dot_general | solution.py:24
  202.9 4.4 convert_element_type.15
  207.3 0.0 reduce-scatter.5.cloned.1.call-update
  207.3 108.8 %reduce-scatter.3.cloned.1.call-done = bf16[128,4096]{1,0:T(8,128)(2,1)} async-done(((bf16[1024,4096]{1,0:T(8,128)(2,1)}), bf16[128,4096]{1,0:T(8,128)(2,1)}) %reduce-scatter.3.cloned.1.call-update) | async-done | bytes 1048592 | tf_op jit(solution)/shard_map/reduce_scatter | solution.py:18
  316.1 2.8 convert_element_type.13
  318.9 128.4 %reduce-scatter.5.cloned.1.call-done = f32[128,512]{1,0:T(8,128)} async-done(((f32[4096,512]{1,0:T(8,128)}), f32[128,512]{1,0:T(8,128)}) %reduce-scatter.5.cloned.1.call-update) | async-done | bytes 262160 | tf_op jit(solution)/shard_map/reduce_scatter | solution.py:28
  447.2 1.7 broadcast_multiply_fusion
Async XLA Ops:
  7.2 72.5 %copy-start = (bf16[1024,512]{1,0:T(8,128)(2,1)S(1)}, bf16[1024,512]{1,0:T(8,128)(2,1)}, u32[]{:S(2)}) copy-start(bf16[1024,512]{1,0:T(8,128)(2,1)} %param.4) | copy-start | bytes 3145732
  7.2 72.5 %all-gather.3.cloned.1.call-start = ((), (), s32[]{:S(2)}) async-start(), calls=%async_computation.2 | async-start | bytes 4325376 | tf_op jit(solution)/shard_map/all_gather | solution.py:14
  7.9 186.6 %all-gather.5.cloned.1.call-start = ((), (), s32[]{:S(2)}) async-start(), calls=%async_computation.4 | async-start | bytes 9437184 | tf_op jit(solution)/shard_map/all_gather | solution.py:21
  8.7 307.4 %reduce-scatter.3.cloned.1.call-start = ((), (), s32[]{:S(2)}) async-start(), calls=%async_computation.3 | async-start | bytes 9437184 | tf_op jit(solution)/shard_map/reduce_scatter | solution.py:18
  88.6 358.6 %reduce-scatter.5.cloned.1.call-start = ((), (), s32[]{:S(2)}) async-start(), calls=%async_computation.5 | async-start | bytes 8650752 | tf_op jit(solution)/shard_map/reduce_scatter | solution.py:28
Sparse Core Ops, SparseCore 0:
  9.9 69.7 all-gather.2
  82.3 112.1 all-gather.4
  198.7 117.4 reduce-scatter.2
  318.5 128.6 reduce-scatter.4
where the time goes:
time: 456 us; the launch traced here: 455 us
  waiting for transfers between devices  415 us (91%)
  matrix products  17.3 us (4%)
  between operations  13.8 us (3%)
  other arithmetic  8.86 us (2%)
    reduce_scatter x1, waiting for transfers between devices, per_device(): lax.psum_scatter(local_term, 'dp', scatter_dimension=0, tiled=True)  128 us
    reduce_scatter x1, waiting for transfers between devices, per_device(): lax.psum_scatter(whole_term.astype(jnp.bfloat16), 'seq', scatter_dimensio...  109 us
    all_gather x1, waiting for transfers between devices, per_device(): gathered = lax.all_gather(acts, 'seq', axis=0, tiled=True)  106 us
    all_gather x1, waiting for transfers between devices, per_device(): full_weight = lax.all_gather(proj_weight, 'dp', axis=0, tiled=True)  71 us
  transfers between devices with their start and end apart: 4, of which 4 were waited for; matrix products, arithmetic and copies ran while one was open for 5% of the time, Pallas kernels for 0%

commit v1 on v0

--- a/solution.py
+++ b/solution.py
@@ -11,7 +11,10 @@
 def per_device(acts, grad_out, proj_weight):
     tok_rows = acts.shape[0]
     total_tokens = tok_rows * lax.axis_size("seq") * lax.axis_size("dp")
-    full_weight = lax.all_gather(proj_weight, "dp", axis=0, tiled=True)
+    devices = lax.axis_size("dp")
+    blocks = jnp.stack([proj_weight for _ in range(devices)])
+    blocks = lax.all_to_all(blocks, "dp", split_axis=0, concat_axis=0)
+    full_weight = jnp.concatenate(blocks, axis=0)
     whole_term = lax.dot_general(
         grad_out, full_weight, (((1,), (1,)), ((), ())), preferred_element_type=jnp.float32
     )

time: 456 us -> 415 us (0.910)
  waiting for transfers between devices: 415 us -> 270 us
  blocking collectives: 0 us -> 105 us
    all_to_all x0 -> x1, blocking collectives: none -> 105 us  [per_device(): blocks = lax.all_to_all(blocks, 'dp', split_axis=0, concat_axis=0)]
    all_gather x1, waiting for transfers between devices: 106 us -> 32.8 us  [per_device(): gathered = lax.all_gather(acts, 'seq', axis=0, tiled=True)]
    all_gather x1 -> x0, waiting for transfers between devices: 71 us -> none  [per_device(): full_weight = lax.all_gather(proj_weight, 'dp', axis=0, tiled=True)]
  transfers between devices with their start and end apart: 4 -> 3, of which waited for: 4 -> 3; matrix products, arithmetic and copies ran while one was open for 5% -> 6% of each run, Pallas kernels for 0% -> 0%
where the time goes in v1:
time: 415 us
  waiting for transfers between devices  270 us (65%)
  blocking collectives  105 us (25%)
  matrix products  15.3 us (4%)
  between operations  13.8 us (3%)
  other arithmetic  8.85 us (2%)
    reduce_scatter x1, waiting for transfers between devices, per_device(): lax.psum_scatter(local_term, 'dp', scatter_dimension=0, tiled=True)  128 us
    reduce_scatter x1, waiting for transfers between devices, per_device(): lax.psum_scatter(whole_term.astype(jnp.bfloat16), 'seq', scatter_dimensio...  108 us
    all_to_all x1, blocking collectives, per_device(): blocks = lax.all_to_all(blocks, 'dp', split_axis=0, concat_axis=0)  105 us
    all_gather x1, waiting for transfers between devices, per_device(): gathered = lax.all_gather(acts, 'seq', axis=0, tiled=True)  32.8 us
    dot_general x1, matrix products, per_device(): lax.dot_general(gathered, grad_out, (((0,), (0,)), ((), ())), preferred_e...  8.39 us
  transfers between devices with their start and end apart: 3, of which 3 were waited for; matrix products, arithmetic and copies ran while one was open for 6% of the time, Pallas kernels for 0%

profile of v1, /device:TPU:4, one launch (start us, length us, event | category | flops | bytes accessed | tf_op | source)
XLA Modules:
  0.0 414.8 jit_solution(2437311945983363870)
XLA Ops:
  7.2 0.0 copy-start
  7.2 0.0 all-gather.2.cloned.1.call-start
  7.2 0.7 all-gather.2.cloned.1.call-update
  7.9 0.0 reduce-scatter.3.cloned.1.call-start
  8.0 1.4 stack.2
  9.3 105.5 %all_to_all.5 = bf16[32,128,512]{2,1,0:T(8,128)(2,1)S(1)} all-to-all(bf16[32,128,512]{2,1,0:T(8,128)(2,1)S(1)} %stack.2), channel_id=1, replica_groups=mesh['dp'=32,'seq'=8] {'dp'}, dimensions={0} | all-to-all | bytes 8388608 | tf_op jit(solution)/shard_map/all_to_all | solution.py:16
  114.8 0.0 copy-done
  114.8 6.9 %convolution_convert_fusion = bf16[1024,4096]{1,0:T(8,128)(2,1)} fusion(bf16[1024,512]{1,0:T(8,128)(2,1)S(1)} %copy-done, bf16[4096,512]{1,0:T(8,128)(2,1)S(1)} %bitcast.5), kind=kOutput, calls=%fused_computation | convolution fusion | flops 4299161600 | bytes 13631488 | tf_op jit(solution)/shard_map/dot_general | solution.py:18
  121.7 0.0 reduce-scatter.3.cloned.1.call-update
  121.7 0.0 reduce-scatter.5.cloned.1.call-start
  121.7 32.8 %all-gather.2.cloned.1.call-done = bf16[1024,4096]{1,0:T(8,128)(2,1)} async-done(((bf16[128,4096]{1,0:T(8,128)(2,1)}), bf16[1024,4096]{1,0:T(8,128)(2,1)}) %all-gather.2.cloned.1.call-update) | async-done | bytes 8388624 | tf_op jit(solution)/shard_map/all_gather | solution.py:24
  154.6 8.4 %convolution_convert_fusion.1 = bf16[4096,512]{1,0:T(8,128)(2,1)S(1)} fusion(bf16[1024,4096]{1,0:T(8,128)(2,1)} %all-gather.2.cloned.1.call-done, bf16[1024,512]{1,0:T(8,128)(2,1)S(1)} %copy-done), kind=kOutput, calls=%fused_computation.1 | convolution fusion | flops 4297064448 | bytes 13631488 | tf_op jit(solution)/shard_map/dot_general | solution.py:27
  163.0 4.4 %convert_element_type.15 = f32[4096,512]{1,0:T(8,128)} convert(bf16[4096,512]{1,0:T(8,128)(2,1)S(1)} %convolution_convert_fusion.1) | non-fusion elementwise | flops 2097152 | bytes 12582912 | tf_op jit(solution)/shard_map/convert_element_type | solution.py:8
  167.4 0.0 reduce-scatter.5.cloned.1.call-update
  167.4 108.3 %reduce-scatter.3.cloned.1.call-done = bf16[128,4096]{1,0:T(8,128)(2,1)} async-done(((bf16[1024,4096]{1,0:T(8,128)(2,1)}), bf16[128,4096]{1,0:T(8,128)(2,1)}) %reduce-scatter.3.cloned.1.call-update) | async-done | bytes 1048592 | tf_op jit(solution)/shard_map/reduce_scatter | solution.py:21
  275.8 2.8 convert_element_type.13
  278.5 128.1 %reduce-scatter.5.cloned.1.call-done = f32[128,512]{1,0:T(8,128)} async-done(((f32[4096,512]{1,0:T(8,128)}), f32[128,512]{1,0:T(8,128)}) %reduce-scatter.5.cloned.1.call-update) | async-done | bytes 262160 | tf_op jit(solution)/shard_map/reduce_scatter | solution.py:31
  406.6 1.7 broadcast_multiply_fusion
Async XLA Ops:
  7.2 107.6 %copy-start = (bf16[1024,512]{1,0:T(8,128)(2,1)S(1)}, bf16[1024,512]{1,0:T(8,128)(2,1)}, u32[]{:S(2)}) copy-start(bf16[1024,512]{1,0:T(8,128)(2,1)} %param.4) | copy-start | bytes 3145732
  7.2 147.4 %all-gather.2.cloned.1.call-start = ((), (), s32[]{:S(2)}) async-start(), calls=%async_computation.4 | async-start | bytes 9437184 | tf_op jit(solution)/shard_map/all_gather | solution.py:24
  7.9 267.9 %reduce-scatter.3.cloned.1.call-start = ((), (), s32[]{:S(2)}) async-start(), calls=%async_computation.3 | async-start | bytes 9437184 | tf_op jit(solution)/shard_map/reduce_scatter | solution.py:21
  121.7 284.9 %reduce-scatter.5.cloned.1.call-start = ((), (), s32[]{:S(2)}) async-start(), calls=%async_computation.5 | async-start | bytes 8650752 | tf_op jit(solution)/shard_map/reduce_scatter | solution.py:31
Sparse Core Ops, SparseCore 0:
  10.6 143.9 all-gather.1
  158.8 116.9 reduce-scatter.2
  278.3 128.2 reduce-scatter.4
